TPU v7x, 256 devices: a whole 4x4x8 slice. The times are simulated.
256 devices in a mesh: rows: 16 (over x, y), cols: 16 (over z, core).
Axes of the slice: x: 4, y: 4, z: 8, core: 2. Of those that a mesh axis runs over, the one named last changes fastest.
Arguments:
- power: float32 [2, 4, 2048, 2048], P(None, None, 'rows', 'cols'), may hold values from -6 to 6
- material: int32 [4, 2048, 2048], P(None, 'rows', 'cols'), may hold values from 0 to 7
- cond_table: float32 [4, 8], replicated, may hold values from 0.5 to 8
- tier_table: int32 [4], replicated, may hold values from 0 to 3
- coarse_slot: int32 [256], replicated, may hold values from 0 to 255, each once
- coarse_inverse: float32 [16, 16, 16], replicated, as said below
Outputs:
- solution: float32 [2, 4, 2048, 2048], P(None, None, 'rows', 'cols')
- residual: float32 [2, 4, 2048, 2048], P(None, None, 'rows', 'cols')
- precond: float32 [2, 4, 2048, 2048], P(None, None, 'rows', 'cols')
Inputs may be any that keep to these rules, and one draw needn't show every extreme that they name: `coarse_slot`: each value once. `coarse_inverse`: symmetric within each owner.
All inputs are finite; a program needn't handle non-finite values.
Results may differ from a plain program's by a relative error of at most 0.0003.
Values sent between devices are 32-bit elements; how exact they have to be, the bound alone decides.
No kernel may reach another device: no remote copies, remote signals or barrier semaphores. Data moves between devices by JAX's collectives and lax.ppermute only.
A program may use at most 64 MiB of HBM per device.

v0:
```python
import math
import jax
import jax.numpy as jnp
from jax import lax
from jax.sharding import PartitionSpec as P

SUB = 128
TIERS = 4
ITERS = 2
SHIFT_C = 0.5
VERT_C = 2.0
SINK_C = 0.05
HIGH = lax.Precision.HIGHEST


def with_halo(cells, sides, width):
    for axis, dim in sides:
        count = lax.axis_size(axis)
        ends = count - 1
        head = lax.slice_in_dim(cells, 0, width, axis=dim)
        tail = lax.slice_in_dim(cells, cells.shape[dim] - width, cells.shape[dim], axis=dim)
        cells = jnp.concatenate(
            [
                lax.ppermute(tail, axis, [(i, (i + 1) % count) for i in range(ends)]),
                cells,
                lax.ppermute(head, axis, [((i + 1) % count, i) for i in range(ends)]),
            ],
            axis=dim,
        )
    return cells


def sine_basis(length):
    counting = jnp.arange(1, length + 1).astype(jnp.float32)
    step_angle = math.pi / (length + 1)
    basis = math.sqrt(2.0 / (length + 1)) * jnp.sin(
        step_angle * counting[:, None] * counting[None, :]
    )
    eigen_values = 2.0 - 2.0 * jnp.cos(step_angle * counting)
    return (basis, eigen_values)


def conductivity(material, cond_table, tier_table):
    tables = cond_table.shape[0]
    picker = (tier_table[:, None] == jnp.arange(tables, dtype=jnp.int32)[None, :]).astype(
        jnp.float32
    )
    tier_rows = jnp.dot(picker, cond_table, precision=HIGH)
    cond = jnp.zeros(material.shape, jnp.float32)
    for number in range(cond_table.shape[1]):
        cond = cond + jnp.where(material == number, tier_rows[:, number][:, None, None], 0.0)
    return (cond, jnp.mean(tier_rows, axis=1))


def coefficients(cond, padded):
    north = 0.5 * (cond + padded[:, :-2, 1:-1])
    south = 0.5 * (cond + padded[:, 2:, 1:-1])
    west = 0.5 * (cond + padded[:, 1:-1, :-2])
    east = 0.5 * (cond + padded[:, 1:-1, 2:])
    upward = VERT_C * 0.5 * (cond[:-1] + cond[1:])
    sink = jnp.concatenate([SINK_C * cond[:1], jnp.zeros_like(cond[1:])], 0)
    return (north, south, west, east, upward, sink)


def operate(temps, padded, coefs):
    north, south, west, east, upward, sink = coefs
    lateral = north * (temps - padded[:, :, :-2, 1:-1]) + south * (temps - padded[:, :, 2:, 1:-1])
    lateral = (
        lateral + west * (temps - padded[:, :, 1:-1, :-2]) + east * (temps - padded[:, :, 1:-1, 2:])
    )
    flux = upward * (temps[:, :-1] - temps[:, 1:])
    zeros_tier = jnp.zeros_like(temps[:, :1])
    vertical = jnp.concatenate([flux, zeros_tier], 1) - jnp.concatenate([zeros_tier, flux], 1)
    return lateral + vertical + sink * temps


def block_solve(temps, basis, denominator):
    shape = temps.shape
    length = basis.shape[0]
    blocks = temps.reshape(
        shape[0], shape[1], shape[2] // length, length, shape[3] // length, length
    )
    spectral = jnp.einsum("ia,vtxayb->vtxiyb", basis, blocks, precision=HIGH)
    spectral = jnp.einsum("vtxiyb,bj->vtxiyj", spectral, basis, precision=HIGH)
    spectral = spectral / denominator[None, :, None, :, None, :]
    result = jnp.einsum("ia,vtxayb->vtxiyb", basis, spectral, precision=HIGH)
    result = jnp.einsum("vtxiyb,bj->vtxiyj", result, basis, precision=HIGH)
    return result.reshape(shape)


def pad_rim(values):
    return with_halo(values, (("rows", 2), ("cols", 3)), 1)


def inner_local(left_arr, right_arr):
    return jnp.sum(left_arr * right_arr, axis=(1, 2, 3))


def shards(power, material, cond_table, tier_table, coarse_slot, coarse_inverse):
    cond, mean_cond = conductivity(material, cond_table, tier_table)
    coefs = coefficients(cond, pad_rim(cond[None])[0])
    basis, eigen_values = sine_basis(SUB)
    denominator = mean_cond[:, None, None] * (
        eigen_values[:, None] + eigen_values[None, :] + SHIFT_C
    )
    half = SUB // 2
    scale = 1.0 / math.sqrt(SUB * SUB * TIERS)
    tile = power.shape[2]
    blocks_side = tile // SUB
    total = coarse_slot.shape[0]
    row_index = lax.axis_index("rows")
    col_index = lax.axis_index("cols")
    row_ids = row_index * blocks_side + jnp.arange(blocks_side, dtype=jnp.int32)
    col_ids = col_index * blocks_side + jnp.arange(blocks_side, dtype=jnp.int32)
    global_ids = (
        row_ids[:, None] * (lax.axis_size("cols") * blocks_side) + col_ids[None, :]
    ).reshape(-1)
    columns = jnp.arange(total, dtype=jnp.int32)
    local_slot = jnp.sum(
        jnp.where(global_ids[:, None] == columns[None, :], coarse_slot[None, :], 0), axis=1
    )
    placer = (local_slot[:, None] == columns[None, :]).astype(jnp.float32)
    owners = coarse_inverse.shape[0]
    own_count = coarse_inverse.shape[1]

    def precondition(resid):
        variants = resid.shape[0]
        aligned = block_solve(resid, basis, denominator)
        extended = with_halo(resid, (("rows", 2), ("cols", 3)), half)
        positions = jnp.arange(tile + SUB, dtype=jnp.int32)
        mask_rows = jnp.where((positions < SUB) & (row_index == 0), 0.0, 1.0)
        mask_cols = jnp.where((positions < SUB) & (col_index == 0), 0.0, 1.0)
        solved_ext = (
            block_solve(extended, basis, denominator) * mask_rows[:, None] * mask_cols[None, :]
        )
        offset = solved_ext[:, :, half : half + tile, half : half + tile]
        sums = (
            resid.reshape(variants, TIERS, blocks_side, SUB, blocks_side, SUB).sum(axis=(1, 3, 5))
            * scale
        )
        ordered = jnp.einsum(
            "sc,vs->cv", placer, sums.reshape(variants, blocks_side * blocks_side), precision=HIGH
        )
        stacked = ordered.reshape(owners, own_count, variants)
        owned = lax.psum_scatter(stacked, "cols", scatter_dimension=0, tiled=True)
        owned = lax.psum(owned, "rows")
        mine = lax.dynamic_slice_in_dim(coarse_inverse, col_index, 1, 0)
        own_sol = jnp.einsum("okj,ojv->okv", mine, owned, precision=HIGH)
        every_sol = lax.all_gather(own_sol, "cols", axis=0, tiled=True)
        picked = jnp.einsum("sc,cv->vs", placer, every_sol.reshape(total, variants), precision=HIGH)
        picked = picked.reshape(variants, 1, blocks_side, 1, blocks_side, 1)
        coarse = jnp.broadcast_to(picked, (variants, TIERS, blocks_side, SUB, blocks_side, SUB))
        return aligned + offset + coarse.reshape(resid.shape) * scale

    solution = jnp.zeros_like(power)
    residual = power
    precond = precondition(residual)
    direction = precond

    def rz_sum(left_arr, right_arr):
        return lax.psum(inner_local(left_arr, right_arr), ("rows", "cols"))

    rz_now = rz_sum(residual, precond)
    for number in range(ITERS):
        image = operate(direction, pad_rim(direction), coefs)
        alpha = rz_now / lax.psum(inner_local(direction, image), ("rows", "cols"))
        solution = solution + alpha[:, None, None, None] * direction
        residual = residual - alpha[:, None, None, None] * image
        precond = precondition(residual)
        rz_next = rz_sum(residual, precond)
        direction = precond + (rz_next / rz_now)[:, None, None, None] * direction
        rz_now = rz_next
    return (solution, residual, precond)


def solution(mesh):
    in_specs = (P(None, None, "rows", "cols"), P(None, "rows", "cols"), P(), P(), P(), P())
    out_specs = (
        P(None, None, "rows", "cols"),
        P(None, None, "rows", "cols"),
        P(None, None, "rows", "cols"),
    )
    return jax.shard_map(shards, mesh=mesh, in_specs=in_specs, out_specs=out_specs, check_vma=False)
```

profile of v0, /device:TPU:1, one launch (start us, length us, event | category | flops | bytes accessed | tf_op | source)
XLA Modules:
  0.0 762.5 jit_solution(1685460788034805416)
XLA Ops:
  4.4 4.7 collective-permute-start
  12.0 4.0 collective-permute-start.4
  18.7 48.1 %all-reduce.5 = f32[16,16,2]{1,2,0:T(2,128)S(1)} all-reduce(f32[16,16,2]{1,2,0:T(2,128)S(1)} %broadcast_multiply_fusion.3), channel_id=5, replica_groups=mesh['rows'=16,'cols'=16] {'cols'}, use_global_device_ids=true, to_apply=%region_3.4.clone | all-reduce | flops 512 | bytes 4096
  68.2 32.1 %psum.49 = f32[16,2]{0,1:T(2,128)S(1)} all-reduce(f32[16,2]{0,1:T(2,128)S(1)} %dynamic-slice_bitcast_fusion.2), channel_id=1, replica_groups=mesh['rows'=16,'cols'=16] {'rows'}, use_global_device_ids=true, to_apply=%region_4.5 | all-reduce | flops 32 | bytes 256 | tf_op jit(solution)/shard_map/psum | solution.py:146
  100.5 24.5 %all-gather.3 = f32[16,16,2]{1,2,0:T(2,128)S(1)} all-gather(f32[1,16,2]{1,2,0:T(2,128)S(1)} %convolution_bitcast_fusion.8), channel_id=2, replica_groups=mesh['rows'=16,'cols'=16] {'cols'}, dimensions={0}, use_global_device_ids=true | all-gather | bytes 2176 | tf_op jit(solution)/shard_map/all_gather | solution.py:149
  161.7 4.1 fusion.8
  174.1 4.0 collective-permute-start.8
  185.6 5.0 collective-permute-start.10
  195.7 78.5 %all-reduce.8 = (f32[2]{0:T(128)S(1)}, f32[2]{0:T(128)S(1)}) all-reduce(f32[2]{0:T(128)S(1)} %get-tuple-element.4, f32[2]{0:T(128)S(1)} %get-tuple-element.3), channel_id=1, replica_groups=mesh['rows'=16,'cols'=16] {'rows','cols'}, use_global_device_ids=true, to_apply=%region_6.7 | all-reduce | flops 4 | bytes 32 | tf_op jit(solution)/shard_map/psum | solution.py:161
  275.4 44.4 %all-reduce.6 = f32[16,16,2]{1,2,0:T(2,128)S(1)} all-reduce(f32[16,16,2]{1,2,0:T(2,128)S(1)} %broadcast_multiply_fusion.2), channel_id=6, replica_groups=mesh['rows'=16,'cols'=16] {'cols'}, use_global_device_ids=true, to_apply=%region_10.11.clone | all-reduce | flops 512 | bytes 4096
  320.5 29.8 %psum.52 = f32[16,2]{0,1:T(2,128)S(1)} all-reduce(f32[16,2]{0,1:T(2,128)S(1)} %dynamic-slice_bitcast_fusion.1), channel_id=1, replica_groups=mesh['rows'=16,'cols'=16] {'rows'}, use_global_device_ids=true, to_apply=%region_11.12 | all-reduce | flops 32 | bytes 256 | tf_op jit(solution)/shard_map/psum | solution.py:146
  351.6 4.0 collective-permute-start.12
  355.8 25.2 %all-gather.4 = f32[16,16,2]{1,2,0:T(2,128)S(1)} all-gather(f32[1,16,2]{1,2,0:T(2,128)S(1)} %convolution_bitcast_fusion.7), channel_id=3, replica_groups=mesh['rows'=16,'cols'=16] {'cols'}, dimensions={0}, use_global_device_ids=true | all-gather | bytes 2176 | tf_op jit(solution)/shard_map/all_gather | solution.py:149
  409.3 5.2 fusion.16
  421.9 4.1 fusion.4
  429.0 3.9 reshape.324
  435.4 74.4 %psum.53 = f32[2]{0:T(128)S(1)} all-reduce(f32[2]{0:T(128)S(1)} %get-tuple-element.53), channel_id=1, replica_groups=mesh['rows'=16,'cols'=16] {'rows','cols'}, use_global_device_ids=true, to_apply=%region_13.14 | all-reduce | flops 2 | bytes 16 | tf_op jit(solution)/shard_map/psum | solution.py:161
  511.3 4.0 collective-permute-start.16
  532.2 78.1 %psum.54 = f32[2]{0:T(128)S(1)} all-reduce(f32[2]{0:T(128)} %get-tuple-element.17), channel_id=1, replica_groups=mesh['rows'=16,'cols'=16] {'rows','cols'}, use_global_device_ids=true, to_apply=%region_15.16 | all-reduce | flops 2 | bytes 16 | tf_op jit(solution)/shard_map/psum | solution.py:166
  614.1 4.0 collective-permute-start.20
  618.2 44.4 %all-reduce.7 = f32[16,16,2]{1,2,0:T(2,128)S(1)} all-reduce(f32[16,16,2]{1,2,0:T(2,128)S(1)} %broadcast_multiply_fusion.1), channel_id=7, replica_groups=mesh['rows'=16,'cols'=16] {'cols'}, use_global_device_ids=true, to_apply=%region_17.18.clone | all-reduce | flops 512 | bytes 4096
  663.3 29.1 %psum.55 = f32[16,2]{0,1:T(2,128)S(1)} all-reduce(f32[16,2]{0,1:T(2,128)S(1)} %dynamic-slice_bitcast_fusion), channel_id=1, replica_groups=mesh['rows'=16,'cols'=16] {'rows'}, use_global_device_ids=true, to_apply=%region_18.19 | all-reduce | flops 32 | bytes 256 | tf_op jit(solution)/shard_map/psum | solution.py:146
  692.5 24.7 %all-gather.5 = f32[16,16,2]{1,2,0:T(2,128)S(1)} all-gather(f32[1,16,2]{1,2,0:T(2,128)S(1)} %convolution_bitcast_fusion.6), channel_id=4, replica_groups=mesh['rows'=16,'cols'=16] {'cols'}, dimensions={0}, use_global_device_ids=true | all-gather | bytes 2176 | tf_op jit(solution)/shard_map/all_gather | solution.py:149
  750.8 3.9 fusion
  (267 shorter events, 176.0 us)
Async XLA Ops:
  3.1 127.2 %collective-permute-start.1 = (f32[2,4,64,128]{2,3,1,0:T(8,128)}, f32[2,4,64,128]{2,3,1,0:T(8,128)S(1)}, u32[]{:S(2)}, u32[]{:S(2)}) collective-permute-start(f32[2,4,64,128]{2,3,1,0:T(8,128)} %get-tuple-element.45), channel_id=1, source_target_pairs={{16,0},{32,16},{48,32},{64,48},{80,64},{96,80},{112,96},{128,112},... | collective-permute-start | bytes 786440 | tf_op jit(solution)/shard_map/ppermute | solution.py:26
  4.4 125.9 %collective-permute-start = (f32[2,4,64,128]{2,3,1,0:T(8,128)}, f32[2,4,64,128]{2,3,1,0:T(8,128)S(1)}, u32[]{:S(2)}, u32[]{:S(2)}) collective-permute-start(f32[2,4,64,128]{2,3,1,0:T(8,128)} %get-tuple-element.44), channel_id=1, source_target_pairs={{0,16},{16,32},{32,48},{48,64},{64,80},{80,96},{96,112},{112,128},... | collective-permute-start | bytes 786440 | tf_op jit(solution)/shard_map/ppermute | solution.py:24
  10.7 125.8 %collective-permute-start.5 = (f32[1,4,1,128]{3,2,1,0:T(1,128)}, f32[1,4,1,128]{3,2,1,0:T(1,128)S(1)}, u32[]{:S(2)}, u32[]{:S(2)}) collective-permute-start(f32[1,4,1,128]{3,2,1,0:T(1,128)} %get-tuple-element.49), channel_id=1, source_target_pairs={{16,0},{32,16},{48,32},{64,48},{80,64},{96,80},{112,96},{128,112},... | collective-permute-start | bytes 6152 | tf_op jit(solution)/shard_map/ppermute | solution.py:26
  12.0 124.5 %collective-permute-start.4 = (f32[1,4,1,128]{3,2,1,0:T(1,128)}, f32[1,4,1,128]{3,2,1,0:T(1,128)S(1)}, u32[]{:S(2)}, u32[]{:S(2)}) collective-permute-start(f32[1,4,1,128]{3,2,1,0:T(1,128)} %get-tuple-element.48), channel_id=1, source_target_pairs={{0,16},{16,32},{32,48},{48,64},{64,80},{80,96},{96,112},{112,128},... | collective-permute-start | bytes 6152 | tf_op jit(solution)/shard_map/ppermute | solution.py:24
  130.9 17.0 %collective-permute-start.3 = (f32[2,4,256,64]{2,3,1,0:T(8,128)S(1)}, f32[2,4,256,64]{2,3,1,0:T(8,128)S(1)}, u32[]{:S(2)}, u32[]{:S(2)}) collective-permute-start(f32[2,4,256,64]{2,3,1,0:T(8,128)S(1)} %get-tuple-element.27), channel_id=1, source_target_pairs={{1,0},{2,1},{3,2},{4,3},{5,4},{6,5},{7,6},{8,7},{9,8},{10,9},{11,1... | collective-permute-start | bytes 1572872 | tf_op jit(solution)/shard_map/ppermute | solution.py:26
  133.0 14.9 %collective-permute-start.2 = (f32[2,4,256,64]{2,3,1,0:T(8,128)S(1)}, f32[2,4,256,64]{2,3,1,0:T(8,128)S(1)}, u32[]{:S(2)}, u32[]{:S(2)}) collective-permute-start(f32[2,4,256,64]{2,3,1,0:T(8,128)S(1)} %get-tuple-element.26), channel_id=1, source_target_pairs={{0,1},{1,2},{2,3},{3,4},{4,5},{5,6},{6,7},{7,8},{8,9},{9,10},{10,1... | collective-permute-start | bytes 1572872 | tf_op jit(solution)/shard_map/ppermute | solution.py:24
  137.8 7.9 %collective-permute-start.7 = (f32[1,4,130,1]{3,2,1,0:T(8,128)S(1)}, f32[1,4,130,1]{3,2,1,0:T(8,128)S(1)}, u32[]{:S(2)}, u32[]{:S(2)}) collective-permute-start(f32[1,4,130,1]{3,2,1,0:T(8,128)S(1)} %get-tuple-element.47), channel_id=1, source_target_pairs={{1,0},{2,1},{3,2},{4,3},{5,4},{6,5},{7,6},{8,7},{9,8},{10,9},{11,1... | collective-permute-start | bytes 6248 | tf_op jit(solution)/shard_map/ppermute | solution.py:26
  139.8 7.1 collective-permute-start.6
  172.8 6.8 collective-permute-start.9
  174.1 5.5 collective-permute-start.8
  182.3 9.1 %collective-permute-start.11 = (f32[2,4,130,1]{2,1,3,0:T(4,128)S(1)}, f32[2,4,130,1]{2,1,3,0:T(4,128)S(1)}, u32[]{:S(2)}, u32[]{:S(2)}) collective-permute-start(f32[2,4,130,1]{2,1,3,0:T(4,128)S(1)} %copy.90), channel_id=1, source_target_pairs={{1,0},{2,1},{3,2},{4,3},{5,4},{6,5},{7,6},{8,7},{9,8},{10,9},{11,1... | collective-permute-start | bytes 12488 | tf_op jit(solution)/shard_map/ppermute | solution.py:26
  185.6 6.8 collective-permute-start.10
  350.3 32.7 %collective-permute-start.13 = (f32[2,4,64,128]{3,2,1,0:T(8,128)S(1)}, f32[2,4,64,128]{3,2,1,0:T(8,128)S(1)}, u32[]{:S(2)}, u32[]{:S(2)}) collective-permute-start(f32[2,4,64,128]{3,2,1,0:T(8,128)S(1)} %get-tuple-element.41), channel_id=1, source_target_pairs={{16,0},{32,16},{48,32},{64,48},{80,64},{96,80},{112,96},{128,112},... | collective-permute-start | bytes 786440 | tf_op jit(solution)/shard_map/ppermute | solution.py:26
  351.6 31.4 %collective-permute-start.12 = (f32[2,4,64,128]{3,2,1,0:T(8,128)S(1)}, f32[2,4,64,128]{3,2,1,0:T(8,128)S(1)}, u32[]{:S(2)}, u32[]{:S(2)}) collective-permute-start(f32[2,4,64,128]{3,2,1,0:T(8,128)S(1)} %get-tuple-element.40), channel_id=1, source_target_pairs={{0,16},{16,32},{32,48},{48,64},{64,80},{80,96},{96,112},{112,128},... | collective-permute-start | bytes 786440 | tf_op jit(solution)/shard_map/ppermute | solution.py:24
  386.8 10.8 %collective-permute-start.15 = (f32[2,4,256,64]{2,3,1,0:T(8,128)}, f32[2,4,256,64]{2,3,1,0:T(8,128)}, u32[]{:S(2)}, u32[]{:S(2)}) collective-permute-start(f32[2,4,256,64]{2,3,1,0:T(8,128)} %copy.97), channel_id=1, source_target_pairs={{1,0},{2,1},{3,2},{4,3},{5,4},{6,5},{7,6},{8,7},{9,8},{10,9},{11,1... | collective-permute-start | bytes 1572872 | tf_op jit(solution)/shard_map/ppermute | solution.py:26
  390.0 9.9 %collective-permute-start.14 = (f32[2,4,256,64]{2,3,1,0:T(8,128)}, f32[2,4,256,64]{2,3,1,0:T(8,128)}, u32[]{:S(2)}, u32[]{:S(2)}) collective-permute-start(f32[2,4,256,64]{2,3,1,0:T(8,128)} %copy.96), channel_id=1, source_target_pairs={{0,1},{1,2},{2,3},{3,4},{4,5},{5,6},{6,7},{7,8},{8,9},{9,10},{10,1... | collective-permute-start | bytes 1572872 | tf_op jit(solution)/shard_map/ppermute | solution.py:24
  510.0 5.3 collective-permute-start.17
  511.3 4.7 collective-permute-start.16
  518.8 8.5 %collective-permute-start.19 = (f32[2,4,130,1]{2,1,3,0:T(4,128)S(1)}, f32[2,4,130,1]{2,1,3,0:T(4,128)S(1)}, u32[]{:S(2)}, u32[]{:S(2)}) collective-permute-start(f32[2,4,130,1]{2,1,3,0:T(4,128)S(1)} %copy.108), channel_id=1, source_target_pairs={{1,0},{2,1},{3,2},{4,3},{5,4},{6,5},{7,6},{8,7},{9,8},{10,9},{11,1... | collective-permute-start | bytes 12488 | tf_op jit(solution)/shard_map/ppermute | solution.py:26
  523.9 4.5 collective-permute-start.18
  612.8 105.6 %collective-permute-start.21 = (f32[2,4,64,128]{3,2,1,0:T(8,128)S(1)}, f32[2,4,64,128]{3,2,1,0:T(8,128)S(1)}, u32[]{:S(2)}, u32[]{:S(2)}) collective-permute-start(f32[2,4,64,128]{3,2,1,0:T(8,128)S(1)} %get-tuple-element.37), channel_id=1, source_target_pairs={{16,0},{32,16},{48,32},{64,48},{80,64},{96,80},{112,96},{128,112},... | collective-permute-start | bytes 786440 | tf_op jit(solution)/shard_map/ppermute | solution.py:26
  614.1 104.4 %collective-permute-start.20 = (f32[2,4,64,128]{3,2,1,0:T(8,128)S(1)}, f32[2,4,64,128]{3,2,1,0:T(8,128)S(1)}, u32[]{:S(2)}, u32[]{:S(2)}) collective-permute-start(f32[2,4,64,128]{3,2,1,0:T(8,128)S(1)} %get-tuple-element.36), channel_id=1, source_target_pairs={{0,16},{16,32},{32,48},{48,64},{64,80},{80,96},{96,112},{112,128},... | collective-permute-start | bytes 786440 | tf_op jit(solution)/shard_map/ppermute | solution.py:24
  720.6 10.7 %collective-permute-start.23 = (f32[2,4,256,64]{2,3,1,0:T(8,128)}, f32[2,4,256,64]{2,3,1,0:T(8,128)S(1)}, u32[]{:S(2)}, u32[]{:S(2)}) collective-permute-start(f32[2,4,256,64]{2,3,1,0:T(8,128)} %copy.115), channel_id=1, source_target_pairs={{1,0},{2,1},{3,2},{4,3},{5,4},{6,5},{7,6},{8,7},{9,8},{10,9},{11,1... | collective-permute-start | bytes 1572872 | tf_op jit(solution)/shard_map/ppermute | solution.py:26
  723.0 9.6 %collective-permute-start.22 = (f32[2,4,256,64]{2,3,1,0:T(8,128)S(1)}, f32[2,4,256,64]{2,3,1,0:T(8,128)}, u32[]{:S(2)}, u32[]{:S(2)}) collective-permute-start(f32[2,4,256,64]{2,3,1,0:T(8,128)S(1)} %copy.114), channel_id=1, source_target_pairs={{0,1},{1,2},{2,3},{3,4},{4,5},{5,6},{6,7},{7,8},{8,9},{9,10},{10,1... | collective-permute-start | bytes 1572872 | tf_op jit(solution)/shard_map/ppermute | solution.py:24
  (53 other events, 1451.8 us)
where the time goes:
time: 770 us; the launch traced here: 762 us
  blocking collectives  534 us (69%)
  matrix products  70.3 us (9%)
  starting transfers between devices  67.9 us (9%)
  local copies, waits for them, and re-layouts  58.5 us (8%)
  other arithmetic  24.1 us (3%)
    psum x2, blocking collectives, rz_sum(): return lax.psum(inner_local(left_arr, right_arr), ('rows', 'cols'))  153 us
    unnamed x3, blocking collectives  137 us
    psum x3, blocking collectives, precondition(): owned = lax.psum(owned, 'rows')  91.1 us
    psum x1, blocking collectives, shards(): alpha = rz_now / lax.psum(inner_local(direction, image), ('rows', 'cols'))  78.1 us
    all_gather x3, blocking collectives, precondition(): every_sol = lax.all_gather(own_sol, 'cols', axis=0, tiled=True)  74.4 us
    ppermute x12, starting transfers between devices, with_halo(): lax.ppermute(tail, axis, [(i, (i + 1) % count) for i in range(ends)])  46.4 us
    ppermute x12, starting transfers between devices, with_halo(): lax.ppermute(head, axis, [((i + 1) % count, i) for i in range(ends)])  21.5 us
    dot_general x6, matrix products, block_solve(): result = jnp.einsum('vtxiyb,bj->vtxiyj', result, basis, precision=HIGH)  20.4 us
  transfers between devices with their start and end apart: 24, of which 7 were waited for; matrix products, arithmetic and copies ran while one was open for 5% of the time, Pallas kernels for 0%

commit v1 on v0

--- a/solution.py
+++ b/solution.py
@@ -158,7 +158,7 @@
     direction = precond
 
     def rz_sum(left_arr, right_arr):
-        return lax.psum(inner_local(left_arr, right_arr), ("rows", "cols"))
+        return lax.psum(lax.psum(inner_local(left_arr, right_arr), "rows"), "cols")
 
     rz_now = rz_sum(residual, precond)
     for number in range(ITERS):

time: 770 us -> 813 us (1.056)
  blocking collectives: 534 us -> 578 us
    psum x1 -> x2, blocking collectives: 78.1 us -> 156 us  [shards(): alpha = rz_now / lax.psum(inner_local(direction, image), ('rows', 'cols'))]
    psum x2 -> x4, blocking collectives: 153 us -> 119 us  [rz_sum(): return lax.psum(lax.psum(inner_local(left_arr, right_arr), 'rows'), 'cols')]
  transfers between devices with their start and end apart: 24 -> 24, of which waited for: 7 -> 7; matrix products, arithmetic and copies ran while one was open for 5% -> 4% of each run, Pallas kernels for 0% -> 0%
where the time goes in v1:
time: 813 us; the launch traced here: 805 us
  blocking collectives  578 us (71%)
  matrix products  70 us (9%)
  starting transfers between devices  67.1 us (8%)
  local copies, waits for them, and re-layouts  57.8 us (7%)
  other arithmetic  24.1 us (3%)
    psum x2, blocking collectives, shards(): alpha = rz_now / lax.psum(inner_local(direction, image), ('rows', 'cols'))  156 us
    unnamed x3, blocking collectives  137 us
    psum x4, blocking collectives, rz_sum(): return lax.psum(lax.psum(inner_local(left_arr, right_arr), 'rows'), 'cols')  119 us
    psum x3, blocking collectives, precondition(): owned = lax.psum(owned, 'rows')  90.6 us
    all_gather x3, blocking collectives, precondition(): every_sol = lax.all_gather(own_sol, 'cols', axis=0, tiled=True)  74.4 us
    ppermute x12, starting transfers between devices, with_halo(): lax.ppermute(tail, axis, [(i, (i + 1) % count) for i in range(ends)])  46 us
    ppermute x12, starting transfers between devices, with_halo(): lax.ppermute(head, axis, [((i + 1) % count, i) for i in range(ends)])  21.1 us
    dot_general x6, matrix products, block_solve(): result = jnp.einsum('vtxiyb,bj->vtxiyj', result, basis, precision=HIGH)  20.4 us
  transfers between devices with their start and end apart: 24, of which 7 were waited for; matrix products, arithmetic and copies ran while one was open for 4% of the time, Pallas kernels for 0%

profile of v1, /device:TPU:1, one launch (start us, length us, event | category | flops | bytes accessed | tf_op | source)
XLA Modules:
  0.0 805.0 jit_solution(3697912469158105041)
XLA Ops:
  4.4 4.7 collective-permute-start
  18.6 48.1 %all-reduce.5 = f32[16,16,2]{1,2,0:T(2,128)S(1)} all-reduce(f32[16,16,2]{1,2,0:T(2,128)S(1)} %broadcast_multiply_fusion.3), channel_id=5, replica_groups=mesh['rows'=16,'cols'=16] {'cols'}, use_global_device_ids=true, to_apply=%region_3.4.clone | all-reduce | flops 512 | bytes 4096
  68.0 32.1 %psum.63 = f32[16,2]{0,1:T(2,128)S(1)} all-reduce(f32[16,2]{0,1:T(2,128)S(1)} %dynamic-slice_bitcast_fusion.2), channel_id=1, replica_groups=mesh['rows'=16,'cols'=16] {'rows'}, use_global_device_ids=true, to_apply=%region_4.5 | all-reduce | flops 32 | bytes 256 | tf_op jit(solution)/shard_map/psum | solution.py:146
  100.3 24.5 %all-gather.3 = f32[16,16,2]{1,2,0:T(2,128)S(1)} all-gather(f32[1,16,2]{1,2,0:T(2,128)S(1)} %convolution_bitcast_fusion.8), channel_id=2, replica_groups=mesh['rows'=16,'cols'=16] {'cols'}, dimensions={0}, use_global_device_ids=true | all-gather | bytes 2176 | tf_op jit(solution)/shard_map/all_gather | solution.py:149
  161.4 4.1 fusion.8
  173.8 4.0 collective-permute-start.8
  185.3 5.0 collective-permute-start.10
  195.4 30.3 %psum.64 = f32[2]{0:T(128)S(1)} all-reduce(f32[2]{0:T(128)S(1)} %get-tuple-element.4), channel_id=1, replica_groups=mesh['rows'=16,'cols'=16] {'rows'}, use_global_device_ids=true, to_apply=%region_6.7 | all-reduce | flops 2 | bytes 16 | tf_op jit(solution)/shard_map/psum | solution.py:161
  225.7 30.0 %psum.65 = f32[2]{0:T(128)S(1)} all-reduce(f32[2]{0:T(128)S(1)} %psum.64), channel_id=1, replica_groups=mesh['rows'=16,'cols'=16] {'cols'}, use_global_device_ids=true, to_apply=%region_7.8 | all-reduce | flops 2 | bytes 16 | tf_op jit(solution)/shard_map/psum | solution.py:161
  255.7 76.4 %psum.66 = f32[2]{0:T(128)S(1)} all-reduce(f32[2]{0:T(128)S(1)} %get-tuple-element.3), channel_id=1, replica_groups=mesh['rows'=16,'cols'=16] {'rows','cols'}, use_global_device_ids=true, to_apply=%region_9.10 | all-reduce | flops 2 | bytes 16 | tf_op jit(solution)/shard_map/psum | solution.py:166
  332.7 45.3 %all-reduce.6 = f32[16,16,2]{1,2,0:T(2,128)S(1)} all-reduce(f32[16,16,2]{1,2,0:T(2,128)S(1)} %broadcast_multiply_fusion.2), channel_id=6, replica_groups=mesh['rows'=16,'cols'=16] {'cols'}, use_global_device_ids=true, to_apply=%region_11.12.clone | all-reduce | flops 512 | bytes 4096
  378.6 29.8 %psum.67 = f32[16,2]{0,1:T(2,128)S(1)} all-reduce(f32[16,2]{0,1:T(2,128)S(1)} %dynamic-slice_bitcast_fusion.1), channel_id=1, replica_groups=mesh['rows'=16,'cols'=16] {'rows'}, use_global_device_ids=true, to_apply=%region_12.13 | all-reduce | flops 32 | bytes 256 | tf_op jit(solution)/shard_map/psum | solution.py:146
  409.8 4.0 collective-permute-start.12
  413.9 25.2 %all-gather.4 = f32[16,16,2]{1,2,0:T(2,128)S(1)} all-gather(f32[1,16,2]{1,2,0:T(2,128)S(1)} %convolution_bitcast_fusion.7), channel_id=3, replica_groups=mesh['rows'=16,'cols'=16] {'cols'}, dimensions={0}, use_global_device_ids=true | all-gather | bytes 2176 | tf_op jit(solution)/shard_map/all_gather | solution.py:149
  467.4 5.2 fusion.16
  480.0 4.1 fusion.4
  493.5 29.0 %psum.68 = f32[2]{0:T(128)S(1)} all-reduce(f32[2]{0:T(128)S(1)} %get-tuple-element.51), channel_id=1, replica_groups=mesh['rows'=16,'cols'=16] {'rows'}, use_global_device_ids=true, to_apply=%region_14.15 | all-reduce | flops 2 | bytes 16 | tf_op jit(solution)/shard_map/psum | solution.py:161
  522.6 30.0 %psum.69 = f32[2]{0:T(128)S(1)} all-reduce(f32[2]{0:T(128)S(1)} %psum.68), channel_id=1, replica_groups=mesh['rows'=16,'cols'=16] {'cols'}, use_global_device_ids=true, to_apply=%region_15.16 | all-reduce | flops 2 | bytes 16 | tf_op jit(solution)/shard_map/psum | solution.py:161
  554.0 4.0 collective-permute-start.16
  574.2 80.1 %psum.70 = f32[2]{0:T(128)S(1)} all-reduce(f32[2]{0:T(128)} %get-tuple-element.15), channel_id=1, replica_groups=mesh['rows'=16,'cols'=16] {'rows','cols'}, use_global_device_ids=true, to_apply=%region_17.18 | all-reduce | flops 2 | bytes 16 | tf_op jit(solution)/shard_map/psum | solution.py:166
  658.0 4.0 collective-permute-start.20
  662.1 43.4 %all-reduce.7 = f32[16,16,2]{1,2,0:T(2,128)S(1)} all-reduce(f32[16,16,2]{1,2,0:T(2,128)S(1)} %broadcast_multiply_fusion.1), channel_id=7, replica_groups=mesh['rows'=16,'cols'=16] {'cols'}, use_global_device_ids=true, to_apply=%region_19.20.clone | all-reduce | flops 512 | bytes 4096
  706.2 28.6 %psum.71 = f32[16,2]{0,1:T(2,128)S(1)} all-reduce(f32[16,2]{0,1:T(2,128)S(1)} %dynamic-slice_bitcast_fusion), channel_id=1, replica_groups=mesh['rows'=16,'cols'=16] {'rows'}, use_global_device_ids=true, to_apply=%region_20.21 | all-reduce | flops 32 | bytes 256 | tf_op jit(solution)/shard_map/psum | solution.py:146
  735.0 24.7 %all-gather.5 = f32[16,16,2]{1,2,0:T(2,128)S(1)} all-gather(f32[1,16,2]{1,2,0:T(2,128)S(1)} %convolution_bitcast_fusion.6), channel_id=4, replica_groups=mesh['rows'=16,'cols'=16] {'cols'}, dimensions={0}, use_global_device_ids=true | all-gather | bytes 2176 | tf_op jit(solution)/shard_map/all_gather | solution.py:149
  (270 shorter events, 186.2 us)
Async XLA Ops:
  3.1 126.8 %collective-permute-start.1 = (f32[2,4,64,128]{2,3,1,0:T(8,128)}, f32[2,4,64,128]{2,3,1,0:T(8,128)S(1)}, u32[]{:S(2)}, u32[]{:S(2)}) collective-permute-start(f32[2,4,64,128]{2,3,1,0:T(8,128)} %get-tuple-element.43), channel_id=1, source_target_pairs={{16,0},{32,16},{48,32},{64,48},{80,64},{96,80},{112,96},{128,112},... | collective-permute-start | bytes 786440 | tf_op jit(solution)/shard_map/ppermute | solution.py:26
  4.4 125.5 %collective-permute-start = (f32[2,4,64,128]{2,3,1,0:T(8,128)}, f32[2,4,64,128]{2,3,1,0:T(8,128)S(1)}, u32[]{:S(2)}, u32[]{:S(2)}) collective-permute-start(f32[2,4,64,128]{2,3,1,0:T(8,128)} %get-tuple-element.42), channel_id=1, source_target_pairs={{0,16},{16,32},{32,48},{48,64},{64,80},{80,96},{96,112},{112,128},... | collective-permute-start | bytes 786440 | tf_op jit(solution)/shard_map/ppermute | solution.py:24
  10.7 125.5 %collective-permute-start.5 = (f32[1,4,1,128]{3,2,1,0:T(1,128)}, f32[1,4,1,128]{3,2,1,0:T(1,128)S(1)}, u32[]{:S(2)}, u32[]{:S(2)}) collective-permute-start(f32[1,4,1,128]{3,2,1,0:T(1,128)} %get-tuple-element.47), channel_id=1, source_target_pairs={{16,0},{32,16},{48,32},{64,48},{80,64},{96,80},{112,96},{128,112},... | collective-permute-start | bytes 6152 | tf_op jit(solution)/shard_map/ppermute | solution.py:26
  12.0 124.2 %collective-permute-start.4 = (f32[1,4,1,128]{3,2,1,0:T(1,128)}, f32[1,4,1,128]{3,2,1,0:T(1,128)S(1)}, u32[]{:S(2)}, u32[]{:S(2)}) collective-permute-start(f32[1,4,1,128]{3,2,1,0:T(1,128)} %get-tuple-element.46), channel_id=1, source_target_pairs={{0,16},{16,32},{32,48},{48,64},{64,80},{80,96},{96,112},{112,128},... | collective-permute-start | bytes 6152 | tf_op jit(solution)/shard_map/ppermute | solution.py:24
  130.5 17.0 %collective-permute-start.3 = (f32[2,4,256,64]{2,3,1,0:T(8,128)S(1)}, f32[2,4,256,64]{2,3,1,0:T(8,128)S(1)}, u32[]{:S(2)}, u32[]{:S(2)}) collective-permute-start(f32[2,4,256,64]{2,3,1,0:T(8,128)S(1)} %get-tuple-element.25), channel_id=1, source_target_pairs={{1,0},{2,1},{3,2},{4,3},{5,4},{6,5},{7,6},{8,7},{9,8},{10,9},{11,1... | collective-permute-start | bytes 1572872 | tf_op jit(solution)/shard_map/ppermute | solution.py:26
  132.6 14.9 %collective-permute-start.2 = (f32[2,4,256,64]{2,3,1,0:T(8,128)S(1)}, f32[2,4,256,64]{2,3,1,0:T(8,128)S(1)}, u32[]{:S(2)}, u32[]{:S(2)}) collective-permute-start(f32[2,4,256,64]{2,3,1,0:T(8,128)S(1)} %get-tuple-element.24), channel_id=1, source_target_pairs={{0,1},{1,2},{2,3},{3,4},{4,5},{5,6},{6,7},{7,8},{8,9},{9,10},{10,1... | collective-permute-start | bytes 1572872 | tf_op jit(solution)/shard_map/ppermute | solution.py:24
  137.5 7.9 collective-permute-start.7
  139.4 7.1 collective-permute-start.6
  172.5 6.8 collective-permute-start.9
  173.8 5.5 collective-permute-start.8
  182.0 9.1 %collective-permute-start.11 = (f32[2,4,130,1]{2,1,3,0:T(4,128)S(1)}, f32[2,4,130,1]{2,1,3,0:T(4,128)S(1)}, u32[]{:S(2)}, u32[]{:S(2)}) collective-permute-start(f32[2,4,130,1]{2,1,3,0:T(4,128)S(1)} %copy.90), channel_id=1, source_target_pairs={{1,0},{2,1},{3,2},{4,3},{5,4},{6,5},{7,6},{8,7},{9,8},{10,9},{11,1... | collective-permute-start | bytes 12488 | tf_op jit(solution)/shard_map/ppermute | solution.py:26
  185.3 6.8 collective-permute-start.10
  408.5 32.7 %collective-permute-start.13 = (f32[2,4,64,128]{3,2,1,0:T(8,128)S(1)}, f32[2,4,64,128]{3,2,1,0:T(8,128)S(1)}, u32[]{:S(2)}, u32[]{:S(2)}) collective-permute-start(f32[2,4,64,128]{3,2,1,0:T(8,128)S(1)} %get-tuple-element.39), channel_id=1, source_target_pairs={{16,0},{32,16},{48,32},{64,48},{80,64},{96,80},{112,96},{128,112},... | collective-permute-start | bytes 786440 | tf_op jit(solution)/shard_map/ppermute | solution.py:26
  409.8 31.4 %collective-permute-start.12 = (f32[2,4,64,128]{3,2,1,0:T(8,128)S(1)}, f32[2,4,64,128]{3,2,1,0:T(8,128)S(1)}, u32[]{:S(2)}, u32[]{:S(2)}) collective-permute-start(f32[2,4,64,128]{3,2,1,0:T(8,128)S(1)} %get-tuple-element.38), channel_id=1, source_target_pairs={{0,16},{16,32},{32,48},{48,64},{64,80},{80,96},{96,112},{112,128},... | collective-permute-start | bytes 786440 | tf_op jit(solution)/shard_map/ppermute | solution.py:24
  444.9 10.8 %collective-permute-start.15 = (f32[2,4,256,64]{2,3,1,0:T(8,128)}, f32[2,4,256,64]{2,3,1,0:T(8,128)}, u32[]{:S(2)}, u32[]{:S(2)}) collective-permute-start(f32[2,4,256,64]{2,3,1,0:T(8,128)} %copy.97), channel_id=1, source_target_pairs={{1,0},{2,1},{3,2},{4,3},{5,4},{6,5},{7,6},{8,7},{9,8},{10,9},{11,1... | collective-permute-start | bytes 1572872 | tf_op jit(solution)/shard_map/ppermute | solution.py:26
  448.1 9.9 %collective-permute-start.14 = (f32[2,4,256,64]{2,3,1,0:T(8,128)}, f32[2,4,256,64]{2,3,1,0:T(8,128)}, u32[]{:S(2)}, u32[]{:S(2)}) collective-permute-start(f32[2,4,256,64]{2,3,1,0:T(8,128)} %copy.96), channel_id=1, source_target_pairs={{0,1},{1,2},{2,3},{3,4},{4,5},{5,6},{6,7},{7,8},{8,9},{9,10},{10,1... | collective-permute-start | bytes 1572872 | tf_op jit(solution)/shard_map/ppermute | solution.py:24
  552.7 5.3 collective-permute-start.17
  554.0 4.7 collective-permute-start.16
  561.4 7.8 collective-permute-start.19
  566.2 4.1 collective-permute-start.18
  656.8 104.1 %collective-permute-start.21 = (f32[2,4,64,128]{3,2,1,0:T(8,128)S(1)}, f32[2,4,64,128]{3,2,1,0:T(8,128)S(1)}, u32[]{:S(2)}, u32[]{:S(2)}) collective-permute-start(f32[2,4,64,128]{3,2,1,0:T(8,128)S(1)} %get-tuple-element.35), channel_id=1, source_target_pairs={{16,0},{32,16},{48,32},{64,48},{80,64},{96,80},{112,96},{128,112},... | collective-permute-start | bytes 786440 | tf_op jit(solution)/shard_map/ppermute | solution.py:26
  658.0 102.8 %collective-permute-start.20 = (f32[2,4,64,128]{3,2,1,0:T(8,128)S(1)}, f32[2,4,64,128]{3,2,1,0:T(8,128)S(1)}, u32[]{:S(2)}, u32[]{:S(2)}) collective-permute-start(f32[2,4,64,128]{3,2,1,0:T(8,128)S(1)} %get-tuple-element.34), channel_id=1, source_target_pairs={{0,16},{16,32},{32,48},{48,64},{64,80},{80,96},{96,112},{112,128},... | collective-permute-start | bytes 786440 | tf_op jit(solution)/shard_map/ppermute | solution.py:24
  763.1 10.7 %collective-permute-start.23 = (f32[2,4,256,64]{2,3,1,0:T(8,128)}, f32[2,4,256,64]{2,3,1,0:T(8,128)S(1)}, u32[]{:S(2)}, u32[]{:S(2)}) collective-permute-start(f32[2,4,256,64]{2,3,1,0:T(8,128)} %copy.115), channel_id=1, source_target_pairs={{1,0},{2,1},{3,2},{4,3},{5,4},{6,5},{7,6},{8,7},{9,8},{10,9},{11,1... | collective-permute-start | bytes 1572872 | tf_op jit(solution)/shard_map/ppermute | solution.py:26
  765.5 9.6 %collective-permute-start.22 = (f32[2,4,256,64]{2,3,1,0:T(8,128)S(1)}, f32[2,4,256,64]{2,3,1,0:T(8,128)}, u32[]{:S(2)}, u32[]{:S(2)}) collective-permute-start(f32[2,4,256,64]{2,3,1,0:T(8,128)S(1)} %copy.114), channel_id=1, source_target_pairs={{0,1},{1,2},{2,3},{3,4},{4,5},{5,6},{6,7},{7,8},{8,9},{9,10},{10,1... | collective-permute-start | bytes 1572872 | tf_op jit(solution)/shard_map/ppermute | solution.py:24
  (53 other events, 1504.6 us)
